TPU v7x, 256 devices: a whole 4x4x8 slice. The times are simulated.
256 devices in a mesh: space: 32 (over z, x), sample: 8 (over y, core).
Axes of the slice: x: 4, y: 4, z: 8, core: 2. Of those that a mesh axis runs over, the one named last changes fastest.
Arguments:
- crops: bfloat16 [256, 16, 64, 1024], P('sample', None, 'space'), may hold values from -6 to 6
- first_kernel: bfloat16 [32, 16, 3, 3, 3], replicated, may hold values from -0.3125 to 0.3125
- second_kernel: bfloat16 [64, 32, 3, 3, 3], replicated, may hold values from -0.21875 to 0.21875
- out_grad: bfloat16 [256, 64, 16, 64], P(('sample', 'space')), may hold values from -0.03125 to 0.03125
Outputs:
- features_out: bfloat16 [256, 64, 16, 64], P(('sample', 'space'))
- first_grad: float32 [32, 16, 3, 3, 3], replicated
- second_grad: float32 [64, 32, 3, 3, 3], replicated
All inputs are finite; a program needn't handle non-finite values.
Results may differ from a plain program's by a relative error of at most 0.012.
Values may be sent and summed in bfloat16 or wider, within the bound.
A program may use at most 128 MiB of HBM per device.

v0:
```python
import jax
import jax.numpy as jnp
from jax import lax
from jax.sharding import PartitionSpec as P

HEIGHT = 8
WIDTH = 128


def forward_conv(field, kernel, depth_pad):
    return lax.conv_general_dilated(
        field,
        kernel,
        (2, 2, 2),
        (depth_pad, (1, 0), (1, 0)),
        dimension_numbers=("NCDHW", "OIDHW", "NCDHW"),
        preferred_element_type=jnp.float32,
    )


def kernel_grad(field, cotangent, depth_pad):
    return lax.conv_general_dilated(
        field,
        cotangent,
        (1, 1, 1),
        (depth_pad, (1, 0), (1, 0)),
        rhs_dilation=(2, 2, 2),
        dimension_numbers=("CNDHW", "IODHW", "CNDHW"),
        preferred_element_type=jnp.float32,
    )


def input_grad(cotangent, kernel):
    flipped = kernel[:, :, ::-1, ::-1, ::-1]
    return lax.conv_general_dilated(
        cotangent,
        flipped,
        (1, 1, 1),
        ((1, 2), (1, 2), (1, 2)),
        lhs_dilation=(2, 2, 2),
        dimension_numbers=("NCDHW", "IODHW", "NCDHW"),
        preferred_element_type=jnp.float32,
    )


def silu_slope(value):
    sigma = jax.nn.sigmoid(value)
    return sigma * (1.0 + value * (1.0 - sigma))


def body(crops, first_kernel, second_kernel, out_grad):
    local_samples, channels_in, planes, flat_cells = crops.shape
    whole_input = lax.all_to_all(crops, "space", split_axis=0, concat_axis=2, tiled=True)
    whole_input = whole_input.reshape(
        whole_input.shape[0], channels_in, whole_input.shape[2], HEIGHT, WIDTH
    )
    first_pre = forward_conv(whole_input, first_kernel, (1, 0))
    act_whole = jax.nn.silu(first_pre).astype(jnp.bfloat16)
    sample_count = act_whole.shape[0]
    second_pre = forward_conv(act_whole, second_kernel, (1, 0))
    features_out = second_pre.astype(jnp.bfloat16).reshape(out_grad.shape)
    cotangent = out_grad.reshape(
        sample_count, out_grad.shape[1], out_grad.shape[2], HEIGHT // 4, WIDTH // 4
    )
    second_grad = kernel_grad(act_whole, cotangent, (1, 0))
    act_grad = input_grad(cotangent, second_kernel).astype(jnp.bfloat16)
    pre_grad = (act_grad.astype(jnp.float32) * silu_slope(first_pre)).astype(jnp.bfloat16)
    first_grad = kernel_grad(whole_input, pre_grad, (1, 0))
    flat = jnp.concatenate([first_grad.reshape(-1), second_grad.reshape(-1)])
    flat = lax.psum(flat, ("space", "sample"))
    first_grad = flat[: first_grad.size].reshape(first_grad.shape)
    second_grad = flat[first_grad.size :].reshape(second_grad.shape)
    return (features_out, first_grad, second_grad)


def solution(mesh):
    placed = (P("sample", None, "space", None), P(), P(), P(("sample", "space"), None, None, None))
    return jax.shard_map(
        body,
        mesh=mesh,
        in_specs=placed,
        out_specs=(P(("sample", "space"), None, None, None), P(), P()),
        check_vma=False,
    )
```

profile of v0, /device:TPU:1, one launch (start us, length us, event | category | flops | bytes accessed | tf_op | source)
XLA Modules:
  0.0 600.1 jit_solution(7680147417381081335)
XLA Ops:
  7.2 12.0 %all-to-all-start = ((bf16[32,16,2,1024]{3,2,1,0:T(2,128)(2,1)}), bf16[32,16,2,1024]{3,2,1,0:T(2,128)(2,1)S(1)}, u32[]{:S(2)}, u32[]{:S(2)}) async-start(bf16[32,16,2,1024]{3,2,1,0:T(2,128)(2,1)} %param.4), calls=%async_computation | async-start | bytes 4194304 | tf_op jit(solution)/shard_map/all_to_all | solution.py:53
  19.3 1.2 copy.80
  20.9 2.5 fusion.19
  23.3 5.4 copy.84
  28.7 38.9 %all-to-all-done = bf16[32,16,2,1024]{3,2,1,0:T(2,128)(2,1)S(1)} async-done(((bf16[32,16,2,1024]{3,2,1,0:T(2,128)(2,1)}), bf16[32,16,2,1024]{3,2,1,0:T(2,128)(2,1)S(1)}, u32[]{:S(2)}, u32[]{:S(2)}) %all-to-all-start) | async-done | bytes 2097184 | tf_op jit(solution)/shard_map/all_to_all | solution.py:53
  69.0 4.9 copy.102
  73.9 5.6 pad.clone
  79.5 32.4 %copy.71 = bf16[16,64,8,1,8,18]{0,4,5,2,1,3:T(8,128)(2,1)} copy(bf16[16,64,8,1,8,18]{1,2,5,4,0,3:T(8,128)(2,1)} %bitcast.50) | data formatting | bytes 4718592 | tf_op jit(solution)/shard_map/conv_general_dilated | solution.py:11
  111.9 3.9 slice.33
  115.8 20.2 %broadcast_select_fusion = (bf16[32,4,8,9,32]{4,2,3,1,0:T(8,128)(2,1)}, bf16[32,4,8,9,32]{4,2,3,1,0:T(8,128)(2,1)}, f32[32,4,8,9,32]{4,2,3,1,0:T(8,128)}) fusion(pred[8,9]{0,1:T(8,128)(4,1)S(1)} %copy-done.4, bf16[32,16,3,3,3]{0,1,4,3,2:T(8,128)(2,1)S(1)} %copy-done.5, bf16[16,64,8,1,7,2]{0,4,5,2,1,3:T(8,128)(2,1)} %slice.33, ...), kind=kOutput, calls=%fused_computation.30 | convolution fusion | flops 241065984 | bytes 4975688 | tf_op jit(solution)/shard_map/conv_general_dilated | solution.py:11
  136.0 2.6 copy.72
  139.1 1.4 copy.74
  140.4 1.0 fusion.48
  142.8 1.8 slice.40
  144.6 1.6 add_multiply_fusion
  146.2 4.8 copy.85
  151.0 11.8 %fusion.9 = f32[64,32,3,3,3]{0,1,4,3,2:T(8,128)S(1)} fusion(bf16[32,4,1,64,32]{4,0,3,1,2:T(8,128)(2,1)} %slice.40, bf16[1,64,16,2,32]{1,4,3,2,0:T(8,128)(2,1)S(1)} %bitcast.62), kind=kOutput, calls=%fused_computation.16 | convolution fusion | flops 91443200 | bytes 876544 | tf_op jit(solution)/shard_map/conv_general_dilated | solution.py:22
  162.9 12.3 %copy.93 = f32[64,32,3,3,3]{4,3,2,1,0:T(4,128)} copy(f32[64,32,3,3,3]{0,1,4,3,2:T(8,128)S(1)} %fusion.9) | data formatting | bytes 442368 | tf_op jit(solution)/shard_map/conv_general_dilated | solution.py:22
  175.2 11.0 %reshape.48 = f32[55296]{0:T(1024)} reshape(f32[64,32,3,3,3]{4,3,2,1,0:T(4,128)} %copy.93) | data formatting | bytes 442368 | tf_op jit(solution)/shard_map/reshape | solution.py:69
  186.1 34.9 %copy.86 = bf16[1,16,64,8,128]{1,0,4,3,2:T(2,128)(2,1)} copy(bf16[1,16,64,8,128]{4,3,1,2,0:T(8,128)(2,1)S(1)} %bitcast.49) | data formatting | bytes 4194304 | tf_op jit(solution)/shard_map/reshape | solution.py:54
  221.0 4.5 fusion.8
  225.5 89.8 %fusion.11 = f32[32,16,3,3,3]{0,1,4,3,2:T(8,128)} fusion(bf16[1,16,64,8,128]{1,0,4,3,2:T(2,128)(2,1)} %copy.86, bf16[32,4,1,64,32]{4,0,3,1,2:T(8,128)(2,1)S(1)} %fusion.8), kind=kOutput, calls=%fused_computation.18 | convolution fusion | flops 204385280 | bytes 2676736 | tf_op jit(solution)/shard_map/conv_general_dilated | solution.py:22
  315.3 4.4 copy.88
  319.7 2.0 reshape.47
  321.7 1.7 pad_maximum_fusion
  323.4 3.5 fusion.26
  327.1 1.1 copy.94
  328.1 239.1 %all-reduce.2.cloned.1.call-done = f32[69120]{0:T(1024)} async-done(((f32[69120]{0:T(1024)}), f32[69120]{0:T(1024)}) %all-reduce.2.cloned.1.call-update) | async-done | bytes 276496 | tf_op jit(solution)/shard_map/psum | solution.py:70
  568.1 1.6 reshape.49
  569.6 2.5 copy.95
  573.1 8.3 %reshape.50 = f32[64,32,3,3,3]{4,3,2,1,0:T(4,128)} reshape(f32[55296]{0:T(1024)S(1)} %slice.42) | data formatting | bytes 442368 | tf_op jit(solution)/shard_map/reshape | solution.py:72
  581.4 11.7 %copy.96 = f32[64,32,3,3,3]{0,1,4,3,2:T(8,128)} copy(f32[64,32,3,3,3]{4,3,2,1,0:T(4,128)} %reshape.50) | data formatting | bytes 442368
  (30 shorter events, 5.4 us)
Async XLA Ops:
  7.2 13.7 %copy-start = (bf16[64,32,3,3,3]{0,1,4,3,2:T(8,128)(2,1)S(1)}, bf16[64,32,3,3,3]{0,1,4,3,2:T(8,128)(2,1)}, u32[]{:S(2)}) copy-start(bf16[64,32,3,3,3]{0,1,4,3,2:T(8,128)(2,1)} %param.6) | copy-start | bytes 331780
  7.2 13.7 %copy-start.3 = (pred[8,10]{0,1:T(8,128)(4,1)S(1)}, pred[8,10]{0,1:T(8,128)(4,1)}, u32[]{:S(2)}) copy-start(pred[8,10]{0,1:T(8,128)(4,1)} %constant.19) | copy-start | bytes 244
  7.2 60.5 %all-to-all-start = ((bf16[32,16,2,1024]{3,2,1,0:T(2,128)(2,1)}), bf16[32,16,2,1024]{3,2,1,0:T(2,128)(2,1)S(1)}, u32[]{:S(2)}, u32[]{:S(2)}) async-start(bf16[32,16,2,1024]{3,2,1,0:T(2,128)(2,1)} %param.4), calls=%async_computation | async-start | bytes 4194304 | tf_op jit(solution)/shard_map/all_to_all | solution.py:53
  19.2 548.0 %all-reduce.2.cloned.1.call-start = ((), (), s32[]{:S(2)}) async-start(), calls=%async_computation.1 | async-start | bytes 557056 | tf_op jit(solution)/shard_map/psum | solution.py:70
  79.5 36.3 %copy-start.4 = (pred[8,9]{0,1:T(8,128)(4,1)S(1)}, pred[8,9]{0,1:T(8,128)(4,1)}, u32[]{:S(2)}) copy-start(pred[8,9]{0,1:T(8,128)(4,1)} %constant.17) | copy-start | bytes 220
  79.5 36.3 %copy-start.5 = (bf16[32,16,3,3,3]{0,1,4,3,2:T(8,128)(2,1)S(1)}, bf16[32,16,3,3,3]{0,1,4,3,2:T(8,128)(2,1)}, u32[]{:S(2)}) copy-start(bf16[32,16,3,3,3]{0,1,4,3,2:T(8,128)(2,1)} %param.5) | copy-start | bytes 82948
  138.6 3.3 copy-start.2
  140.4 1.5 copy-start.1
  141.9 2.7 slice-start
  141.9 2.7 slice-start.1
Sparse Core Ops, SparseCore 0:
  323.5 243.6 all-reduce.1
where the time goes:
time: 607 us; the launch traced here: 600 us
  waiting for transfers between devices  278 us (46%)
  local copies, waits for them, and re-layouts  160 us (26%)
  matrix products  128 us (21%)
  between operations  14.4 us (2%)
  starting transfers between devices  12.1 us (2%)
  other arithmetic  7.78 us (1%)
    psum x1, waiting for transfers between devices, body(): flat = lax.psum(flat, ('space', 'sample'))  239 us
    conv_general_dilated x2, matrix products, kernel_grad(): lax.conv_general_dilated(field, cotangent, (1, 1, 1), (depth_pad, (1, 0),...  102 us
    reshape x2, local copies, waits for them, and re-layouts, body(): whole_input.reshape(whole_input.shape[0], channels_in, whole_input.shape[...  40.5 us
    all_to_all x1, waiting for transfers between devices, body(): lax.all_to_all(crops, 'space', split_axis=0, concat_axis=2, tiled=True)  38.9 us
    conv_general_dilated x2, local copies, waits for them, and re-layouts, forward_conv(): lax.conv_general_dilated(field, kernel, (2, 2, 2), (depth_pad, (1, 0), (1...  36.3 us
    conv_general_dilated x2, matrix products, forward_conv(): lax.conv_general_dilated(field, kernel, (2, 2, 2), (depth_pad, (1, 0), (1...  23.7 us
    unnamed x23, local copies, waits for them, and re-layouts  22.7 us
    conv_general_dilated x2, local copies, waits for them, and re-layouts, kernel_grad(): lax.conv_general_dilated(field, cotangent, (1, 1, 1), (depth_pad, (1, 0),...  16.7 us
  transfers between devices with their start and end apart: 2, of which 2 were waited for; matrix products, arithmetic and copies ran while one was open for 2% of the time, Pallas kernels for 0%

commit v1 on v0

--- a/solution.py
+++ b/solution.py
@@ -5,6 +5,11 @@
 
 HEIGHT = 8
 WIDTH = 128
+
+
+def by_each_axis(array, inner_axis, outer_axis):
+    partial = lax.psum(array, inner_axis)
+    return lax.psum(partial, outer_axis)
 
 
 def forward_conv(field, kernel, depth_pad):
@@ -67,7 +72,7 @@
     pre_grad = (act_grad.astype(jnp.float32) * silu_slope(first_pre)).astype(jnp.bfloat16)
     first_grad = kernel_grad(whole_input, pre_grad, (1, 0))
     flat = jnp.concatenate([first_grad.reshape(-1), second_grad.reshape(-1)])
-    flat = lax.psum(flat, ("space", "sample"))
+    flat = by_each_axis(flat, "space", "sample")
     first_grad = flat[: first_grad.size].reshape(first_grad.shape)
     second_grad = flat[first_grad.size :].reshape(second_grad.shape)
     return (features_out, first_grad, second_grad)

time: 607 us -> 565 us (0.931)
  waiting for transfers between devices: 278 us -> 238 us
    psum x1 -> x2, waiting for transfers between devices: 239 us -> 199 us  [the longest x1 135 us: by_each_axis(): partial = lax.psum(array, inner_axis)]
    unnamed x23 -> x19, local copies, waits for them, and re-layouts: 22.7 us -> 22.3 us
  transfers between devices with their start and end apart: 2 -> 3, of which waited for: 2 -> 3; matrix products, arithmetic and copies ran while one was open for 2% -> 3% of each run, Pallas kernels for 0% -> 0%
where the time goes in v1:
time: 565 us; the launch traced here: 559 us
  waiting for transfers between devices  238 us (42%)
  local copies, waits for them, and re-layouts  161 us (28%)
  matrix products  126 us (22%)
  between operations  14.4 us (3%)
  starting transfers between devices  12.1 us (2%)
  other arithmetic  7.78 us (1%)
    psum x1, waiting for transfers between devices, by_each_axis(): partial = lax.psum(array, inner_axis)  135 us
    conv_general_dilated x2, matrix products, kernel_grad(): lax.conv_general_dilated(field, cotangent, (1, 1, 1), (depth_pad, (1, 0),...  101 us
    psum x1, waiting for transfers between devices, by_each_axis(): return lax.psum(partial, outer_axis)  64.2 us
    reshape x2, local copies, waits for them, and re-layouts, body(): whole_input.reshape(whole_input.shape[0], channels_in, whole_input.shape[...  40.7 us
    all_to_all x1, waiting for transfers between devices, body(): lax.all_to_all(crops, 'space', split_axis=0, concat_axis=2, tiled=True)  39 us
    conv_general_dilated x2, local copies, waits for them, and re-layouts, forward_conv(): lax.conv_general_dilated(field, kernel, (2, 2, 2), (depth_pad, (1, 0), (1...  36.2 us
    unnamed x19, local copies, waits for them, and re-layouts  22.3 us
    conv_general_dilated x2, matrix products, forward_conv(): lax.conv_general_dilated(field, kernel, (2, 2, 2), (depth_pad, (1, 0), (1...  21.9 us
  transfers between devices with their start and end apart: 3, of which 3 were waited for; matrix products, arithmetic and copies ran while one was open for 3% of the time, Pallas kernels for 0%

profile of v1, /device:TPU:1, one launch (start us, length us, event | category | flops | bytes accessed | tf_op | source)
XLA Modules:
  0.0 558.9 jit_solution(3667440024557366543)
XLA Ops:
  7.2 12.0 %all-to-all-start = ((bf16[32,16,2,1024]{3,2,1,0:T(2,128)(2,1)}), bf16[32,16,2,1024]{3,2,1,0:T(2,128)(2,1)S(1)}, u32[]{:S(2)}, u32[]{:S(2)}) async-start(bf16[32,16,2,1024]{3,2,1,0:T(2,128)(2,1)} %param.4), calls=%async_computation | async-start | bytes 4194304 | tf_op jit(solution)/shard_map/all_to_all | solution.py:58
  19.3 1.2 copy.80
  20.9 2.5 fusion.19
  23.3 5.4 copy.84
  28.7 39.0 %all-to-all-done = bf16[32,16,2,1024]{3,2,1,0:T(2,128)(2,1)S(1)} async-done(((bf16[32,16,2,1024]{3,2,1,0:T(2,128)(2,1)}), bf16[32,16,2,1024]{3,2,1,0:T(2,128)(2,1)S(1)}, u32[]{:S(2)}, u32[]{:S(2)}) %all-to-all-start) | async-done | bytes 2097184 | tf_op jit(solution)/shard_map/all_to_all | solution.py:58
  69.0 4.9 copy.102
  73.9 5.6 %pad.clone = bf16[16,64,8,1,144]{1,2,4,0,3:T(8,128)(2,1)} pad(bf16[16,64,8,1,128]{1,2,4,0,3:T(8,128)(2,1)} %copy.102, bf16[]{:T(256)} %constant.6), padding=0_0x0_0x0_0x0_0x1_15 | pad | bytes 4456450 | tf_op jit(solution)/shard_map/reshape | solution.py:59
  79.6 32.5 %copy.71 = bf16[16,64,8,1,8,18]{0,4,5,2,1,3:T(8,128)(2,1)} copy(bf16[16,64,8,1,8,18]{1,2,5,4,0,3:T(8,128)(2,1)} %bitcast.50) | data formatting | bytes 4718592 | tf_op jit(solution)/shard_map/conv_general_dilated | solution.py:16
  112.0 3.8 slice.33
  115.8 20.1 %broadcast_select_fusion = (bf16[32,4,8,9,32]{4,2,3,1,0:T(8,128)(2,1)}, bf16[32,4,8,9,32]{4,2,3,1,0:T(8,128)(2,1)}, f32[32,4,8,9,32]{4,2,3,1,0:T(8,128)}) fusion(pred[8,9]{0,1:T(8,128)(4,1)S(1)} %copy-done.2, bf16[32,16,3,3,3]{0,1,4,3,2:T(8,128)(2,1)S(1)} %copy-done.3, bf16[16,64,8,1,7,2]{0,4,5,2,1,3:T(8,128)(2,1)} %slice.33, ...), kind=kOutput, calls=%fused_computation.30 | convolution fusion | flops 241065984 | bytes 4975688 | tf_op jit(solution)/shard_map/conv_general_dilated | solution.py:16
  136.0 2.7 copy.89
  138.7 1.8 slice.40
  140.4 1.6 add_multiply_fusion
  142.1 4.9 copy.85
  146.9 11.8 %fusion.9 = f32[64,32,3,3,3]{0,1,4,3,2:T(8,128)S(1)} fusion(bf16[32,4,1,64,32]{4,0,3,1,2:T(8,128)(2,1)} %slice.40, bf16[1,64,16,2,32]{1,4,3,2,0:T(8,128)(2,1)S(1)} %bitcast.62), kind=kOutput, calls=%fused_computation.16 | convolution fusion | flops 91443200 | bytes 876544 | tf_op jit(solution)/shard_map/conv_general_dilated | solution.py:27
  158.8 12.2 %copy.93 = f32[64,32,3,3,3]{4,3,2,1,0:T(4,128)} copy(f32[64,32,3,3,3]{0,1,4,3,2:T(8,128)S(1)} %fusion.9) | data formatting | bytes 442368 | tf_op jit(solution)/shard_map/conv_general_dilated | solution.py:27
  171.0 11.0 %reshape.48 = f32[55296]{0:T(1024)} reshape(f32[64,32,3,3,3]{4,3,2,1,0:T(4,128)} %copy.93) | data formatting | bytes 442368 | tf_op jit(solution)/shard_map/reshape | solution.py:74
  181.9 35.0 %copy.86 = bf16[1,16,64,8,128]{1,0,4,3,2:T(2,128)(2,1)} copy(bf16[1,16,64,8,128]{4,3,1,2,0:T(8,128)(2,1)S(1)} %bitcast.49) | data formatting | bytes 4194304 | tf_op jit(solution)/shard_map/reshape | solution.py:59
  217.0 4.5 fusion.8
  221.5 89.6 %fusion.11 = f32[32,16,3,3,3]{0,1,4,3,2:T(8,128)} fusion(bf16[1,16,64,8,128]{1,0,4,3,2:T(2,128)(2,1)} %copy.86, bf16[32,4,1,64,32]{4,0,3,1,2:T(8,128)(2,1)S(1)} %fusion.8), kind=kOutput, calls=%fused_computation.18 | convolution fusion | flops 204385280 | bytes 2676736 | tf_op jit(solution)/shard_map/conv_general_dilated | solution.py:27
  311.1 4.6 copy.88
  315.6 2.0 reshape.47
  317.6 1.7 pad_maximum_fusion
  319.4 2.6 copy.72
  322.4 1.4 copy.74
  323.9 134.8 %all-reduce.3.cloned.1.call-done = f32[69120]{0:T(1024)} async-done(((f32[69120]{0:T(1024)}), f32[69120]{0:T(1024)}) %all-reduce.3.cloned.1.call-update) | async-done | bytes 276496 | tf_op jit(solution)/shard_map/psum | solution.py:11
  458.7 1.8 fusion.26
  461.8 64.2 %all-reduce.5.cloned.1.call-done = f32[69120]{0:T(1024)} async-done(((f32[69120]{0:T(1024)}), f32[69120]{0:T(1024)}) %all-reduce.5.cloned.1.call-update) | async-done | bytes 276496 | tf_op jit(solution)/shard_map/psum | solution.py:12
  526.9 1.6 reshape.49
  528.4 2.5 copy.95
  531.9 8.3 %reshape.50 = f32[64,32,3,3,3]{4,3,2,1,0:T(4,128)} reshape(f32[55296]{0:T(1024)S(1)} %slice.42) | data formatting | bytes 442368 | tf_op jit(solution)/shard_map/reshape | solution.py:77
  540.2 11.7 %copy.96 = f32[64,32,3,3,3]{0,1,4,3,2:T(8,128)} copy(f32[64,32,3,3,3]{4,3,2,1,0:T(4,128)} %reshape.50) | data formatting | bytes 442368
  (29 shorter events, 5.4 us)
Async XLA Ops:
  7.2 13.7 %copy-start = (bf16[64,32,3,3,3]{0,1,4,3,2:T(8,128)(2,1)S(1)}, bf16[64,32,3,3,3]{0,1,4,3,2:T(8,128)(2,1)}, u32[]{:S(2)}) copy-start(bf16[64,32,3,3,3]{0,1,4,3,2:T(8,128)(2,1)} %param.6) | copy-start | bytes 331780
  7.2 13.7 %copy-start.1 = (pred[8,10]{0,1:T(8,128)(4,1)S(1)}, pred[8,10]{0,1:T(8,128)(4,1)}, u32[]{:S(2)}) copy-start(pred[8,10]{0,1:T(8,128)(4,1)} %constant.19) | copy-start | bytes 244
  7.2 60.5 %all-to-all-start = ((bf16[32,16,2,1024]{3,2,1,0:T(2,128)(2,1)}), bf16[32,16,2,1024]{3,2,1,0:T(2,128)(2,1)S(1)}, u32[]{:S(2)}, u32[]{:S(2)}) async-start(bf16[32,16,2,1024]{3,2,1,0:T(2,128)(2,1)} %param.4), calls=%async_computation | async-start | bytes 4194304 | tf_op jit(solution)/shard_map/all_to_all | solution.py:58
  19.2 439.5 %all-reduce.3.cloned.1.call-start = ((), (), s32[]{:S(2)}) async-start(), calls=%async_computation.1 | async-start | bytes 557056 | tf_op jit(solution)/shard_map/psum | solution.py:11
  79.6 36.3 %copy-start.2 = (pred[8,9]{0,1:T(8,128)(4,1)S(1)}, pred[8,9]{0,1:T(8,128)(4,1)}, u32[]{:S(2)}) copy-start(pred[8,9]{0,1:T(8,128)(4,1)} %constant.17) | copy-start | bytes 220
  79.6 36.3 %copy-start.3 = (bf16[32,16,3,3,3]{0,1,4,3,2:T(8,128)(2,1)S(1)}, bf16[32,16,3,3,3]{0,1,4,3,2:T(8,128)(2,1)}, u32[]{:S(2)}) copy-start(bf16[32,16,3,3,3]{0,1,4,3,2:T(8,128)(2,1)} %param.5) | copy-start | bytes 82948
  135.9 4.5 slice-start
  135.9 4.5 slice-start.1
  319.3 206.7 %all-reduce.5.cloned.1.call-start = ((), (), s32[]{:S(2)}) async-start(), calls=%async_computation.2 | async-start | bytes 557056 | tf_op jit(solution)/shard_map/psum | solution.py:12
Sparse Core Ops, SparseCore 0:
  319.5 139.1 all-reduce.2
  461.0 64.9 all-reduce.4
